TPU v7x, 32 devices: a whole 2x2x4 slice. The times are simulated.
32 devices in a mesh: col: 8 (over z, x), row: 4 (over y, core).
Axes of the slice: x: 2, y: 2, z: 4, core: 2. Of those that a mesh axis runs over, the one named last changes fastest.
Arguments:
- weight: float32 [8192, 16384], P('row', 'col'), may hold values from -6 to 6
- momentum: float32 [8192, 16384], P('row', 'col'), may hold values from -6 to 6
- gradient: bfloat16 [8192, 16384], P('row', 'col'), may hold values from -6 to 6
- right_factor: float32 [16384, 256], P('col'), may hold values from -6 to 6
Outputs:
- new_weight: float32 [8192, 16384], P('row', 'col')
- new_momentum: float32 [8192, 16384], P('row', 'col')
- new_factor: float32 [16384, 256], P('col')
All inputs are finite; a program needn't handle non-finite values.
Results may differ from a plain program's by a relative error of at most 0.0003.
Values sent between devices are 32-bit elements; how exact they have to be, the bound alone decides.
No kernel may reach another device: no remote copies, remote signals or barrier semaphores. Data moves between devices by JAX's collectives and lax.ppermute only.
A program may use at most 128 MiB of HBM per device.

v0:
```python
import jax
import jax.numpy as jnp
from jax import lax
from jax.sharding import PartitionSpec as P

D_IN = 16384


def contract(first, second, first_dim, second_dim):
    return lax.dot_general(
        first,
        second,
        (((first_dim,), (second_dim,)), ((), ())),
        precision=lax.Precision.HIGHEST,
        preferred_element_type=jnp.float32,
    )


def orthonormal(left_raw, gram_matrix):
    lower = jnp.linalg.cholesky(gram_matrix)
    return lax.linalg.triangular_solve(
        lower, left_raw, left_side=False, lower=True, transpose_a=True
    )


def on_device(weight, momentum, gradient, right_factor):
    combined = momentum + gradient.astype(jnp.float32)
    partial_value = contract(combined, right_factor, 1, 0)
    left_raw = lax.psum(partial_value, "col")
    gram_matrix = lax.psum(contract(left_raw, left_raw, 0, 0), "row")
    left_factor = orthonormal(left_raw, gram_matrix)
    right_raw = lax.psum(contract(combined, left_factor, 0, 0), "row")
    squares = lax.psum(jnp.sum(right_raw * right_raw, axis=0), "col")
    new_factor = right_raw / jnp.sqrt(squares / D_IN + 1e-06)
    new_momentum = combined - 0.05 * contract(left_factor, right_raw, 1, 1)
    new_weight = weight - 0.5 * contract(left_factor, new_factor, 1, 1)
    return (new_weight, new_momentum, new_factor)


def solution(mesh):
    in_specs = (P("row", "col"), P("row", "col"), P("row", "col"), P("col", None))
    out_specs = (P("row", "col"), P("row", "col"), P("col", None))
    return jax.shard_map(
        on_device, mesh=mesh, in_specs=in_specs, out_specs=out_specs, check_vma=False
    )
```

profile of v0, /device:TPU:0, one launch (start us, length us, event | category | flops | bytes accessed | tf_op | source)
XLA Modules:
  0.0 417.1 jit_solution(15536495732991310134)
XLA Ops:
  7.2 1.5 copy-done
  8.8 18.3 %fusion.1 = f32[2048,256]{1,0:T(8,128)} fusion(f32[2048,256]{1,0:T(8,128)S(1)} %copy-done, f32[2048,2048]{1,0:T(8,128)} %param.5, bf16[2048,2048]{1,0:T(8,128)(2,1)} %param.6), kind=kOutput, calls=%fused_computation.6 | convolution fusion | flops 12893290496 | bytes 29360128 | tf_op jit(solution)/shard_map/dot_general | solution.py:10
  27.1 105.1 %all-reduce.5.cloned.1.call-done = f32[2048,256]{1,0:T(8,128)} async-done(((f32[2048,256]{1,0:T(8,128)}), f32[2048,256]{1,0:T(8,128)}) %all-reduce.5.cloned.1.call-update) | async-done | bytes 2097168 | tf_op jit(solution)/shard_map/psum | solution.py:29
  132.2 6.4 %fusion.14 = f32[256,256]{0,1:T(8,128)} fusion(f32[2048,256]{1,0:T(8,128)} %all-reduce.5.cloned.1.call-done), kind=kOutput, calls=%fused_computation.40 | convolution fusion | flops 1610612736 | bytes 2359296 | tf_op jit(solution)/shard_map/dot_general | solution.py:10
  138.9 31.5 %all-reduce.7.cloned.1.call-done = f32[256,256]{0,1:T(8,128)} async-done(((f32[256,256]{0,1:T(8,128)}), f32[256,256]{0,1:T(8,128)}) %all-reduce.7.cloned.1.call-update) | async-done | bytes 262160 | tf_op jit(solution)/shard_map/psum | solution.py:30
  170.3 1.1 copy.8
  171.4 1.0 fusion.4
  172.4 11.7 %cholesky.50 = f32[128,128]{1,0:T(8,128)S(1)} custom-call(f32[128,128]{1,0:T(8,128)S(1)} %cholesky.118), custom_call_target="Cholesky" | custom-call | tf_op jit(solution)/shard_map/jit(cholesky)/cholesky | solution.py:20
  184.2 9.8 %custom-call.14 = f32[1,128,128]{1,2,0:T(8,128)S(1)} custom-call(f32[1,128,128]{2,1,0:T(8,128)S(1)} %get-tuple-element.24), custom_call_target="InvertDiagBlocksLowerTriangular" | custom-call | tf_op jit(solution)/shard_map/jit(cholesky)/cholesky | solution.py:20
  194.5 11.7 %cholesky.105 = f32[128,128]{1,0:T(8,128)S(1)} custom-call(f32[128,128]{1,0:T(8,128)S(1)} %convolution_subtract_fusion.1), custom_call_target="Cholesky" | custom-call | tf_op jit(solution)/shard_map/jit(cholesky)/cholesky | solution.py:20
  208.3 4.2 %while.1 = (s32[]{:T(128)}, f32[256,256]{1,0:T(8,128)S(1)}, s32[2,2]{1,0:T(2,128)S(1)}, f32[2,128,128]{2,1,0:T(8,128)S(1)}, s32[]{:T(128)}) while((s32[]{:T(128)}, f32[256,256]{1,0:T(8,128)S(1)}, s32[2,2]{1,0:T(2,128)S(1)}, f32[2,128,128]{2,1,0:T(8,128)S(1)}, s32[]{:T(128)}) %tuple.27), condition=%wide.while_cond, body=%wide.while_body.sunk | while | flops 2 | bytes 131189 | solution.py:21
  209.1 1.4 bitcast_dynamic-update-slice_fusion.2
  211.1 1.4 bitcast_dynamic-update-slice_fusion.2
  212.5 19.7 %custom-call.15 = f32[2,128,128]{1,2,0:T(8,128)S(1)} custom-call(f32[2,128,128]{2,1,0:T(8,128)S(1)} %get-tuple-element.10), custom_call_target="InvertDiagBlocksLowerTriangular" | custom-call | tf_op jit(solution)/shard_map/triangular_solve | solution.py:21
  232.2 1.1 fusion.2
  233.3 1.8 convolution_subtract_fusion
  235.1 1.1 fusion.5
  236.2 32.4 %fusion = f32[2048,256]{1,0:T(8,128)} fusion(f32[2048,2048]{1,0:T(8,128)} %param.5, bf16[2048,2048]{1,0:T(8,128)(2,1)} %param.6, f32[2048,128]{0,1:T(8,128)S(1)} %fusion.5, f32[2048,128]{0,1:T(8,128)S(1)} %fusion.2), kind=kOutput, calls=%fused_computation.5 | convolution fusion | flops 12893814784 | bytes 29360128 | tf_op jit(solution)/shard_map/dot_general | solution.py:10
  268.6 51.5 %all-reduce.9.cloned.1.call-done = f32[2048,256]{1,0:T(8,128)} async-done(((f32[2048,256]{1,0:T(8,128)}), f32[2048,256]{1,0:T(8,128)}) %all-reduce.9.cloned.1.call-update) | async-done | bytes 2097168 | tf_op jit(solution)/shard_map/psum | solution.py:32
  320.2 2.0 multiply_reduce_fusion
  322.2 21.3 %psum.31 = f32[256]{0:T(256)S(1)} all-reduce(f32[256]{0:T(256)S(1)} %multiply_reduce_fusion), channel_id=1, replica_groups=mesh['col'=8,'row'=4] {'col'}, use_global_device_ids=true, to_apply=%region_8.9 | all-reduce | flops 256 | bytes 2048 | tf_op jit(solution)/shard_map/psum | solution.py:33
  343.7 1.3 copy-done.7
  345.2 31.9 %multiply_subtract_fusion.1 = f32[2048,2048]{1,0:T(8,128)} fusion(f32[2048,2048]{1,0:T(8,128)} %param.4, f32[2048,256]{1,0:T(8,128)S(1)} %broadcast_divide_fusion, f32[2048,128]{0,1:T(8,128)S(1)} %copy-done.6, f32[2048,128]{0,1:T(8,128)S(1)} %fusion.2), kind=kOutput, calls=%fused_computation.3 | convolution fusion | flops 12893814784 | bytes 37748736 | tf_op jit(solution)/shard_map/dot_general | solution.py:10
  377.1 33.3 %multiply_subtract_fusion = f32[2048,2048]{1,0:T(8,128)} fusion(f32[2048,256]{1,0:T(8,128)S(1)} %copy-done.4, f32[2048,2048]{1,0:T(8,128)} %param.5, bf16[2048,2048]{1,0:T(8,128)(2,1)} %param.6, f32[2048,128]{0,1:T(8,128)S(1)} %copy-done.6, f32[2048,128]{0,1:T(8,128)S(1)} %fusion.2), kind=kOutput, calls=%fused_computation.2 | convolution fusion | flops 12902203392 | bytes 46137344 | tf_op jit(solution)/shard_map/dot_general | solution.py:10
  (37 shorter events, 3.1 us)
Async XLA Ops:
  7.2 1.6 copy-start
  7.2 125.1 %all-reduce.5.cloned.1.call-start = ((), (), s32[]{:S(2)}) async-start(), calls=%async_computation | async-start | bytes 4194304 | tf_op jit(solution)/shard_map/psum | solution.py:29
  27.0 143.3 %all-reduce.7.cloned.1.call-start = ((), (), s32[]{:S(2)}) async-start(), calls=%async_computation.1 | async-start | bytes 524288 | tf_op jit(solution)/shard_map/psum | solution.py:30
  138.6 93.6 %copy-start.2 = (f32[2048,256]{1,0:T(8,128)S(1)}, f32[2048,256]{1,0:T(8,128)}, u32[]{:S(2)}) copy-start(f32[2048,256]{1,0:T(8,128)} %all-reduce.5.cloned.1.call-done) | copy-start | bytes 6291460
  138.6 181.5 %all-reduce.9.cloned.1.call-start = ((), (), s32[]{:S(2)}) async-start(), calls=%async_computation.2 | async-start | bytes 4194304 | tf_op jit(solution)/shard_map/psum | solution.py:32
  236.2 32.4 %copy-start.5 = (f32[2048,128]{0,1:T(8,128)}, f32[2048,128]{0,1:T(8,128)S(1)}, u32[]{:S(2)}) copy-start(f32[2048,128]{0,1:T(8,128)S(1)} %fusion.5) | copy-start | bytes 3145732
  320.2 23.4 %copy-start.3 = (f32[2048,256]{1,0:T(8,128)S(1)}, f32[2048,256]{1,0:T(8,128)}, u32[]{:S(2)}) copy-start(f32[2048,256]{1,0:T(8,128)} %all-reduce.9.cloned.1.call-done) | copy-start | bytes 6291460
  343.6 1.6 copy-start.6
  343.7 1.3 copy-start.7
  345.2 31.9 %copy-start.4 = (f32[2048,256]{1,0:T(8,128)S(1)}, f32[2048,256]{1,0:T(8,128)}, u32[]{:S(2)}) copy-start(f32[2048,256]{1,0:T(8,128)} %all-reduce.9.cloned.1.call-done) | copy-start | bytes 6291460
  377.1 33.3 %copy-start.1 = (f32[2048,256]{1,0:T(8,128)S(1)}, f32[2048,256]{1,0:T(8,128)}, u32[]{:S(2)}) copy-start(f32[2048,256]{1,0:T(8,128)} %param.7) | copy-start | bytes 6291460
Sparse Core Ops, SparseCore 0:
  27.2 105.0 all-reduce.4
  138.8 31.5 all-reduce.6
  268.8 51.3 all-reduce.8
where the time goes:
time: 424 us; the launch traced here: 417 us
  waiting for transfers between devices  188 us (44%)
  matrix products  127 us (30%)
  other arithmetic  56.8 us (13%)
  blocking collectives  21.3 us (5%)
  between operations  15.4 us (4%)
  local copies, waits for them, and re-layouts  8.11 us (2%)
    dot_general x5, matrix products, contract(): lax.dot_general(first, second, (((first_dim,), (second_dim,)), ((), ())),...  122 us
    psum x1, waiting for transfers between devices, on_device(): left_raw = lax.psum(partial_value, 'col')  105 us
    psum x1, waiting for transfers between devices, on_device(): right_raw = lax.psum(contract(combined, left_factor, 0, 0), 'row')  51.5 us
    another operation x6, other arithmetic, orthonormal(): lower = jnp.linalg.cholesky(gram_matrix)  34 us
    psum x1, waiting for transfers between devices, on_device(): gram_matrix = lax.psum(contract(left_raw, left_raw, 0, 0), 'row')  31.5 us
    psum x1, blocking collectives, on_device(): squares = lax.psum(jnp.sum(right_raw * right_raw, axis=0), 'col')  21.3 us
    another operation x3, other arithmetic, orthonormal(): lax.linalg.triangular_solve(lower, left_raw, left_side=False, lower=True,...  19.7 us
  transfers between devices with their start and end apart: 3, of which 3 were waited for; matrix products, arithmetic and copies ran while one was open for 0% of the time, Pallas kernels for 0%

commit v1 on v0

--- a/solution.py
+++ b/solution.py
@@ -26,7 +26,7 @@
 def on_device(weight, momentum, gradient, right_factor):
     combined = momentum + gradient.astype(jnp.float32)
     partial_value = contract(combined, right_factor, 1, 0)
-    left_raw = lax.psum(partial_value, "col")
+    left_raw = jnp.sum(lax.all_gather(partial_value, "col"), axis=0)
     gram_matrix = lax.psum(contract(left_raw, left_raw, 0, 0), "row")
     left_factor = orthonormal(left_raw, gram_matrix)
     right_raw = lax.psum(contract(combined, left_factor, 0, 0), "row")

time: 424 us -> 562 us (1.33)
  waiting for transfers between devices: 188 us -> 312 us
  other arithmetic: 56.8 us -> 64 us
  matrix products: 127 us -> 133 us
    all_gather x0 -> x1, waiting for transfers between devices: none -> 230 us  [on_device(): left_raw = jnp.sum(lax.all_gather(partial_value, 'col'), axis=0)]
    psum x1 -> x0, waiting for transfers between devices: 105 us -> none  [on_device(): left_raw = lax.psum(partial_value, 'col')]
    reduce_sum x0 -> x1, other arithmetic: none -> 7.14 us  [on_device(): left_raw = jnp.sum(lax.all_gather(partial_value, 'col'), axis=0)]
    dot_general x5, matrix products: 122 us -> 129 us  [contract(): lax.dot_general(first, second, (((first_dim,), (second_dim,)), ((), ())),...]
where the time goes in v1:
time: 562 us; the launch traced here: 555 us
  waiting for transfers between devices  312 us (56%)
  matrix products  133 us (24%)
  other arithmetic  64 us (11%)
  blocking collectives  21.3 us (4%)
  between operations  15.7 us (3%)
  local copies, waits for them, and re-layouts  8.11 us (1%)
    all_gather x1, waiting for transfers between devices, on_device(): left_raw = jnp.sum(lax.all_gather(partial_value, 'col'), axis=0)  230 us
    dot_general x5, matrix products, contract(): lax.dot_general(first, second, (((first_dim,), (second_dim,)), ((), ())),...  129 us
    psum x1, waiting for transfers between devices, on_device(): right_raw = lax.psum(contract(combined, left_factor, 0, 0), 'row')  51.5 us
    another operation x6, other arithmetic, orthonormal(): lower = jnp.linalg.cholesky(gram_matrix)  33.9 us
    psum x1, waiting for transfers between devices, on_device(): gram_matrix = lax.psum(contract(left_raw, left_raw, 0, 0), 'row')  30.3 us
    psum x1, blocking collectives, on_device(): squares = lax.psum(jnp.sum(right_raw * right_raw, axis=0), 'col')  21.3 us
    another operation x3, other arithmetic, orthonormal(): lax.linalg.triangular_solve(lower, left_raw, left_side=False, lower=True,...  19.7 us
  transfers between devices with their start and end apart: 3, of which 3 were waited for; matrix products, arithmetic and copies ran while one was open for 0% of the time, Pallas kernels for 0%

profile of v1, /device:TPU:0, one launch (start us, length us, event | category | flops | bytes accessed | tf_op | source)
XLA Modules:
  0.0 554.7 jit_solution(12251417694212683297)
XLA Ops:
  7.2 1.5 copy-done
  8.8 18.2 %fusion.1 = f32[2048,256]{1,0:T(8,128)} fusion(f32[2048,256]{1,0:T(8,128)S(1)} %copy-done, f32[2048,2048]{1,0:T(8,128)} %param.5, bf16[2048,2048]{1,0:T(8,128)(2,1)} %param.6), kind=kOutput, calls=%fused_computation.6 | convolution fusion | flops 12893290496 | bytes 29360128 | tf_op jit(solution)/shard_map/dot_general | solution.py:10
  27.1 230.1 %all-gather.3.cloned.1.call-done = f32[16384,256]{1,0:T(8,128)} async-done(((f32[2048,256]{1,0:T(8,128)}), f32[16384,256]{1,0:T(8,128)}) %all-gather.3.cloned.1.call-update) | async-done | bytes 16777232 | tf_op jit(solution)/shard_map/all_gather | solution.py:29
  257.2 7.1 %reduce_sum.18 = f32[2048,256]{1,0:T(8,128)S(1)} reduce(f32[8,2048,256]{2,1,0:T(8,128)} %bitcast.37, f32[]{:T(128)} %constant.77.clone.1), dimensions={0}, to_apply=%region_0.0 | reduce | flops 3670016 | bytes 18874372 | tf_op jit(solution)/shard_map/reduce_sum | solution.py:29
  264.3 4.2 fusion.14
  268.9 30.3 %all-reduce.4.cloned.1.call-done = f32[256,256]{0,1:T(8,128)} async-done(((f32[256,256]{0,1:T(8,128)}), f32[256,256]{0,1:T(8,128)}) %all-reduce.4.cloned.1.call-update) | async-done | bytes 262160 | tf_op jit(solution)/shard_map/psum | solution.py:30
  299.2 1.1 copy.8
  301.2 11.7 %cholesky.50 = f32[128,128]{1,0:T(8,128)S(1)} custom-call(f32[128,128]{1,0:T(8,128)S(1)} %cholesky.118), custom_call_target="Cholesky" | custom-call | tf_op jit(solution)/shard_map/jit(cholesky)/cholesky | solution.py:20
  313.0 9.8 %custom-call.14 = f32[1,128,128]{1,2,0:T(8,128)S(1)} custom-call(f32[1,128,128]{2,1,0:T(8,128)S(1)} %get-tuple-element.24), custom_call_target="InvertDiagBlocksLowerTriangular" | custom-call | tf_op jit(solution)/shard_map/jit(cholesky)/cholesky | solution.py:20
  323.3 11.7 %cholesky.105 = f32[128,128]{1,0:T(8,128)S(1)} custom-call(f32[128,128]{1,0:T(8,128)S(1)} %convolution_subtract_fusion.1), custom_call_target="Cholesky" | custom-call | tf_op jit(solution)/shard_map/jit(cholesky)/cholesky | solution.py:20
  337.1 4.0 while.1
  337.7 1.4 bitcast_dynamic-update-slice_fusion.2
  339.7 1.4 bitcast_dynamic-update-slice_fusion.2
  341.1 19.7 %custom-call.15 = f32[2,128,128]{1,2,0:T(8,128)S(1)} custom-call(f32[2,128,128]{2,1,0:T(8,128)S(1)} %get-tuple-element.10), custom_call_target="InvertDiagBlocksLowerTriangular" | custom-call | tf_op jit(solution)/shard_map/triangular_solve | solution.py:21
  360.8 1.1 fusion.2
  361.9 1.8 convolution_subtract_fusion
  363.7 1.1 fusion.5
  364.8 41.1 %fusion = f32[2048,256]{1,0:T(8,128)} fusion(f32[2048,2048]{1,0:T(8,128)} %param.5, bf16[2048,2048]{1,0:T(8,128)(2,1)} %param.6, f32[2048,128]{0,1:T(8,128)S(1)} %fusion.5, f32[2048,128]{0,1:T(8,128)S(1)} %fusion.2), kind=kOutput, calls=%fused_computation.5 | convolution fusion | flops 12893814784 | bytes 29360128 | tf_op jit(solution)/shard_map/dot_general | solution.py:10
  406.0 51.5 %all-reduce.6.cloned.1.call-done = f32[2048,256]{1,0:T(8,128)} async-done(((f32[2048,256]{1,0:T(8,128)}), f32[2048,256]{1,0:T(8,128)}) %all-reduce.6.cloned.1.call-update) | async-done | bytes 2097168 | tf_op jit(solution)/shard_map/psum | solution.py:32
  457.5 2.0 multiply_reduce_fusion
  459.5 21.3 %psum.23 = f32[256]{0:T(256)S(1)} all-reduce(f32[256]{0:T(256)S(1)} %multiply_reduce_fusion), channel_id=1, replica_groups=mesh['col'=8,'row'=4] {'col'}, use_global_device_ids=true, to_apply=%region_8.9 | all-reduce | flops 256 | bytes 2048 | tf_op jit(solution)/shard_map/psum | solution.py:33
  481.1 1.3 copy-done.6
  482.5 31.9 %multiply_subtract_fusion.1 = f32[2048,2048]{1,0:T(8,128)} fusion(f32[2048,2048]{1,0:T(8,128)} %param.4, f32[2048,256]{1,0:T(8,128)S(1)} %broadcast_divide_fusion, f32[2048,128]{0,1:T(8,128)S(1)} %copy-done.5, f32[2048,128]{0,1:T(8,128)S(1)} %fusion.2), kind=kOutput, calls=%fused_computation.3 | convolution fusion | flops 12893814784 | bytes 37748736 | tf_op jit(solution)/shard_map/dot_general | solution.py:10
  514.4 33.4 %multiply_subtract_fusion = f32[2048,2048]{1,0:T(8,128)} fusion(f32[2048,256]{1,0:T(8,128)S(1)} %copy-done.3, f32[2048,2048]{1,0:T(8,128)} %param.5, bf16[2048,2048]{1,0:T(8,128)(2,1)} %param.6, f32[2048,128]{0,1:T(8,128)S(1)} %copy-done.5, f32[2048,128]{0,1:T(8,128)S(1)} %fusion.2), kind=kOutput, calls=%fused_computation.2 | convolution fusion | flops 12902203392 | bytes 46137344 | tf_op jit(solution)/shard_map/dot_general | solution.py:10
  (36 shorter events, 4.2 us)
Async XLA Ops:
  7.2 1.6 copy-start
  7.2 250.0 %all-gather.3.cloned.1.call-start = ((), (), s32[]{:S(2)}) async-start(), calls=%async_computation.2 | async-start | bytes 18874368 | tf_op jit(solution)/shard_map/all_gather | solution.py:29
  27.0 272.1 %all-reduce.4.cloned.1.call-start = ((), (), s32[]{:S(2)}) async-start(), calls=%async_computation | async-start | bytes 524288 | tf_op jit(solution)/shard_map/psum | solution.py:30
  268.5 189.0 %all-reduce.6.cloned.1.call-start = ((), (), s32[]{:S(2)}) async-start(), calls=%async_computation.1 | async-start | bytes 4194304 | tf_op jit(solution)/shard_map/psum | solution.py:32
  364.8 41.1 %copy-start.4 = (f32[2048,128]{0,1:T(8,128)}, f32[2048,128]{0,1:T(8,128)S(1)}, u32[]{:S(2)}) copy-start(f32[2048,128]{0,1:T(8,128)S(1)} %fusion.5) | copy-start | bytes 3145732
  457.5 23.4 %copy-start.2 = (f32[2048,256]{1,0:T(8,128)S(1)}, f32[2048,256]{1,0:T(8,128)}, u32[]{:S(2)}) copy-start(f32[2048,256]{1,0:T(8,128)} %all-reduce.6.cloned.1.call-done) | copy-start | bytes 6291460
  480.9 1.6 copy-start.5
  481.0 1.3 copy-start.6
  482.5 31.9 %copy-start.3 = (f32[2048,256]{1,0:T(8,128)S(1)}, f32[2048,256]{1,0:T(8,128)}, u32[]{:S(2)}) copy-start(f32[2048,256]{1,0:T(8,128)} %all-reduce.6.cloned.1.call-done) | copy-start | bytes 6291460
  514.4 33.4 %copy-start.1 = (f32[2048,256]{1,0:T(8,128)S(1)}, f32[2048,256]{1,0:T(8,128)}, u32[]{:S(2)}) copy-start(f32[2048,256]{1,0:T(8,128)} %param.7) | copy-start | bytes 6291460
Sparse Core Ops, SparseCore 0:
  27.2 229.9 all-gather.2
  268.6 30.4 all-reduce.3
  406.1 51.3 all-reduce.5
